TPU v7x, 256 devices: a whole 4x4x8 slice. The times are simulated.
256 devices in a mesh: azim: 32 (over y_hi, z, core), beam: 2 (over y_lo), sweep: 4 (over x).
Axes of the slice: x: 4, y: 4 (y_hi: 2, y_lo: 2; y = y_hi * 2 + y_lo), z: 8, core: 2. Of those that a mesh axis runs over, the one named last changes fastest.
Arguments:
- features: bfloat16 [2048, 4, 4, 256], P('azim', 'sweep', 'beam'), may hold values from -16 to 16
- cotangent: bfloat16 [2048, 4, 4, 256], P('azim', 'sweep', 'beam'), may hold values from -6 to 6
- w_query: bfloat16 [256, 256], replicated
- w_key: bfloat16 [256, 256], replicated
- w_value: bfloat16 [256, 256], replicated, may hold values from -0.375 to 0.375
- w_out: bfloat16 [256, 256], replicated, may hold values from -0.375 to 0.375
- w_conv: bfloat16 [256, 27, 256], replicated, may hold values from -0.078125 to 0.078125
- sector_mask: int32 [32, 32], replicated, may hold values from 0 to 1, as said below
Outputs:
- features_grad: bfloat16 [2048, 4, 4, 256], P('azim', 'sweep', 'beam')
- weight_grads: float32 [256, 31, 256], P('azim', None, ('beam', 'sweep'))
Inputs may be any that keep to these rules, and one draw needn't show every extreme that they name: `sector_mask`: entry [i, j] is 1 where query sector i may attend to key sector j, else 0; every diagonal entry is 1.
All inputs are finite; a program needn't handle non-finite values.
Results may differ from a plain program's by a relative error of at most 0.012.
The roundings to bfloat16 on the way count: a program that leaves them out, or rounds other values in their place, can miss the bound.
Values may be sent and summed in bfloat16 or wider, within the bound.
A program may use at most 128 MiB of HBM per device.

v0:
```python
import jax
import jax.numpy as jnp
from jax import lax
from jax.sharding import PartitionSpec as P

HEADS = 8
SECTOR = 64
TAPS = 27
highest = lax.Precision.HIGHEST
masked_score = -1e30


def padded_2(block, sides, width):
    for axis, dim in sides:
        count = lax.axis_size(axis)
        forward = [(i, i + 1) for i in range(count - 1)]
        forward.append((count - 1, 0))
        backward = [(target, source) for source, target in forward]
        low = lax.ppermute(
            lax.slice_in_dim(block, block.shape[dim] - width, None, axis=dim), axis, forward
        )
        high = lax.ppermute(lax.slice_in_dim(block, 0, width, axis=dim), axis, backward)
        block = jnp.concatenate([low, block, high], axis=dim)
    return block


def sector_onehot(first_row, row_total, sectors):
    sector_of = (first_row + jnp.arange(row_total, dtype=jnp.int32)) // SECTOR
    return (sector_of[:, None] == jnp.arange(sectors, dtype=jnp.int32)[None, :]).astype(jnp.float32)


def allowed_table(sector_mask, query_first, query_total, key_first, key_total):
    sectors = sector_mask.shape[0]
    query_hot = sector_onehot(query_first, query_total, sectors)
    key_hot = sector_onehot(key_first, key_total, sectors)
    lookup = jnp.dot(jnp.dot(query_hot, sector_mask.astype(jnp.float32)), key_hot.T)
    return lookup > 0.5


def split_heads(tensor):
    return tensor.reshape(tensor.shape[:3] + (HEADS, tensor.shape[3] // HEADS))


def project(flat_rows, weight):
    return jnp.dot(flat_rows, weight, preferred_element_type=jnp.float32).astype(jnp.bfloat16)


def scores_of(queries, key_rows, allowed):
    score_scale = (queries.shape[3] // HEADS) ** (-0.5)
    raw_scores = jnp.einsum(
        "asbhe,ksbhe->sbhak",
        split_heads(queries),
        split_heads(key_rows),
        preferred_element_type=jnp.float32,
    )
    return jnp.where(allowed, raw_scores * score_scale, masked_score)


def key_side(queries, grad_attended, logsum, row_delta, key_rows, value_rows, allowed):
    score_scale = (queries.shape[3] // HEADS) ** (-0.5)
    scores = scores_of(queries, key_rows, allowed)
    weights_full = jnp.where(allowed, jnp.exp(scores - logsum[..., None]), 0.0)
    grad_prob = jnp.einsum(
        "asbhe,ksbhe->sbhak",
        split_heads(grad_attended),
        split_heads(value_rows),
        preferred_element_type=jnp.float32,
    )
    grad_score = (weights_full * (grad_prob - row_delta[..., None])).astype(jnp.bfloat16)
    grad_key = (
        jnp.einsum(
            "sbhak,asbhe->ksbhe",
            grad_score,
            split_heads(queries),
            preferred_element_type=jnp.float32,
        )
        * score_scale
    )
    grad_value = jnp.einsum(
        "sbhak,asbhe->ksbhe",
        weights_full.astype(jnp.bfloat16),
        split_heads(grad_attended),
        preferred_element_type=jnp.float32,
    )
    return (grad_key.reshape(key_rows.shape), grad_value.reshape(key_rows.shape))


def edge_factors(position, devices, length):
    lower_keep = jnp.where(position > 0, 1.0, 0.0).astype(jnp.bfloat16)
    upper_keep = jnp.where(position < devices - 1, 1.0, 0.0).astype(jnp.bfloat16)
    middle = jnp.ones((length,), jnp.bfloat16)
    return jnp.concatenate([lower_keep[None], middle, upper_keep[None]])


def gather_taps(padded, col_count, sweeps, beam_rows, direction):
    pieces = []
    for offset_one in (-1, 0, 1):
        for offset_two in (-1, 0, 1):
            for offset_three in (-1, 0, 1):
                first_at = 1 + direction * offset_one
                second_at = 1 + direction * offset_two
                third_at = 1 + direction * offset_three
                pieces.append(
                    padded[
                        first_at : first_at + col_count,
                        second_at : second_at + sweeps,
                        third_at : third_at + beam_rows,
                    ]
                )
    return jnp.stack(pieces, axis=3)


def per_device(features, cotangent, w_query, w_key, w_value, w_out, w_conv, sector_mask):
    col_count, sweeps, beam_rows, channels = features.shape
    row_count = col_count * sweeps * beam_rows
    flat_in = features.reshape(row_count, channels)
    keep_edges = (
        edge_factors(lax.axis_index("sweep"), lax.axis_size("sweep"), sweeps)[:, None, None]
        * edge_factors(lax.axis_index("beam"), lax.axis_size("beam"), beam_rows)[None, :, None]
    )
    queries = project(flat_in, w_query).reshape(features.shape)
    key_proj = project(flat_in, w_key).reshape(features.shape)
    values = project(flat_in, w_value).reshape(features.shape)
    col_first = lax.axis_index("azim") * col_count
    key_all, value_all = (
        lax.all_gather(key_proj, "azim", axis=0, tiled=True),
        lax.all_gather(values, "azim", axis=0, tiled=True),
    )
    allowed_all = allowed_table(sector_mask, col_first, col_count, 0, key_all.shape[0])
    scores = scores_of(queries, key_all, allowed_all)
    peak_score = jnp.max(scores, axis=-1)
    logsum = peak_score + jnp.log(jnp.sum(jnp.exp(scores - peak_score[..., None]), axis=-1))
    weights_full = jnp.where(allowed_all, jnp.exp(scores - logsum[..., None]), 0.0)
    attended = jnp.einsum(
        "sbhak,ksbhe->asbhe",
        weights_full.astype(jnp.bfloat16),
        split_heads(value_all),
        preferred_element_type=jnp.float32,
    )
    attended = attended.reshape(features.shape).astype(jnp.bfloat16)
    attended_flat = attended.reshape(row_count, channels)
    mixed_out = flat_in.astype(jnp.float32) + jnp.dot(
        attended_flat, w_out, preferred_element_type=jnp.float32
    )
    layer_out = mixed_out.reshape(features.shape).astype(jnp.bfloat16)
    both_pad = (
        padded_2(jnp.stack([layer_out, cotangent]), (("azim", 1), ("beam", 3), ("sweep", 2)), 1)
        * keep_edges
    )
    layer_pad = both_pad[0]
    cot_pad = both_pad[1]
    cot_flat = cotangent.reshape(row_count, channels)
    cot_taps = gather_taps(cot_pad, col_count, sweeps, beam_rows, -1).reshape(
        row_count, TAPS, channels
    )
    grad_layer = cot_flat.astype(jnp.float32) + jnp.einsum(
        "nto,ito->ni", cot_taps, w_conv, preferred_element_type=jnp.float32
    )
    layer_taps = gather_taps(layer_pad, col_count, sweeps, beam_rows, 1).reshape(
        row_count, TAPS, channels
    )
    grad_layer_bf = grad_layer.astype(jnp.bfloat16)
    grad_attended = (
        jnp.dot(grad_layer_bf, w_out.T, preferred_element_type=jnp.float32)
        .astype(jnp.bfloat16)
        .reshape(features.shape)
    )
    row_delta = jnp.einsum(
        "asbhe,asbhe->sbha",
        split_heads(grad_attended),
        split_heads(attended),
        preferred_element_type=jnp.float32,
    )
    grad_prob = jnp.einsum(
        "asbhe,ksbhe->sbhak",
        split_heads(grad_attended),
        split_heads(value_all),
        preferred_element_type=jnp.float32,
    )
    grad_score = (weights_full * (grad_prob - row_delta[..., None])).astype(jnp.bfloat16)
    score_scale = (channels // HEADS) ** (-0.5)
    grad_query = (
        jnp.einsum(
            "sbhak,ksbhe->asbhe",
            grad_score,
            split_heads(key_all),
            preferred_element_type=jnp.float32,
        )
        * score_scale
    )
    grad_query = grad_query.reshape(row_count, channels)
    allowed = allowed_table(
        sector_mask, col_first, col_count, jnp.int32(0), lax.axis_size("azim") * col_count
    )
    grad_key_part, grad_value_part = key_side(
        queries, grad_attended, logsum, row_delta, key_all, value_all, allowed
    )
    key_grads = lax.psum_scatter(
        jnp.concatenate([grad_key_part, grad_value_part], axis=3),
        "azim",
        scatter_dimension=0,
        tiled=True,
    )
    grad_key = key_grads[..., :channels]
    grad_value = key_grads[..., channels:]
    grad_key_flat = grad_key.reshape(row_count, channels)
    grad_value_flat = grad_value.reshape(row_count, channels)
    grad_in = grad_layer + jnp.dot(grad_query, w_query.astype(jnp.float32).T, precision=highest)
    grad_in = grad_in + jnp.dot(grad_key_flat, w_key.astype(jnp.float32).T, precision=highest)
    grad_in = grad_in + jnp.dot(grad_value_flat, w_value.astype(jnp.float32).T, precision=highest)
    features_grad = grad_in.astype(jnp.bfloat16).reshape(features.shape)
    flat_wide = flat_in.astype(jnp.float32)
    projection_terms = jnp.stack(
        [
            jnp.einsum("ni,no->io", flat_wide, grad_query, precision=highest),
            jnp.einsum("ni,no->io", flat_wide, grad_key_flat, precision=highest),
            jnp.einsum("ni,no->io", flat_wide, grad_value_flat, precision=highest),
            jnp.einsum(
                "ni,no->io", attended_flat, grad_layer_bf, preferred_element_type=jnp.float32
            ),
        ],
        axis=1,
    )
    conv_terms = jnp.einsum("nti,no->ito", layer_taps, cot_flat, preferred_element_type=jnp.float32)
    weight_rows = lax.psum_scatter(
        jnp.concatenate([projection_terms, conv_terms], axis=1),
        "azim",
        scatter_dimension=0,
        tiled=True,
    )
    weight_grads = lax.psum_scatter(weight_rows, ("beam", "sweep"), scatter_dimension=2, tiled=True)
    return (features_grad, weight_grads)


def solution(mesh):
    in_specs = (
        P("azim", "sweep", "beam", None),
        P("azim", "sweep", "beam", None),
        P(),
        P(),
        P(),
        P(),
        P(),
        P(),
    )
    out_specs = (P("azim", "sweep", "beam", None), P("azim", None, ("beam", "sweep")))
    return jax.shard_map(
        per_device, mesh=mesh, in_specs=in_specs, out_specs=out_specs, check_vma=False
    )
```

profile of v0, /device:TPU:32, one launch (start us, length us, event | category | flops | bytes accessed | tf_op | source)
XLA Modules:
  0.0 751.3 jit_solution(16207301087636658915)
XLA Ops:
  7.2 1.6 reshape.290
  8.9 1.7 convolution_convert_fusion.2
  12.2 1.7 convolution_convert_fusion.4
  17.0 1.7 convolution_convert_fusion.3
  18.7 1.7 reshape.293
  20.4 1.8 copy.106
  22.3 2.0 convolution_compare_fusion
  24.3 69.6 %all-gather.5.cloned.1.call-done = bf16[2048,1,2,256]{3,2,1,0:T(2,128)(2,1)} async-done(((bf16[64,1,2,256]{3,2,1,0:T(2,128)(2,1)}), bf16[2048,1,2,256]{3,2,1,0:T(2,128)(2,1)}) %all-gather.5.cloned.1.call-update) | async-done | bytes 2097168 | tf_op jit(solution)/shard_map/all_gather | solution.py:126
  94.0 6.2 copy.105
  100.2 3.4 fusion.1
  103.6 2.2 exponential_reduce_fusion
  106.9 66.8 %all-gather.3.cloned.1.call-done = bf16[2048,1,2,256]{3,2,1,0:T(2,128)(2,1)} async-done(((bf16[64,1,2,256]{3,2,1,0:T(2,128)(2,1)}), bf16[2048,1,2,256]{3,2,1,0:T(2,128)(2,1)}) %all-gather.3.cloned.1.call-update) | async-done | bytes 2097168 | tf_op jit(solution)/shard_map/all_gather | solution.py:127
  173.7 6.2 copy.103
  179.9 6.8 convolution_convert_fusion
  186.7 1.8 copy.107
  188.5 1.8 convert_element_type.105
  190.3 1.7 fusion.7
  197.4 1.5 collective-permute-done.1
  198.9 1.7 collective-permute-done
  204.3 1.7 collective-permute-done.3
  206.8 1.7 pad_maximum_fusion.1
  208.4 2.7 collective-permute-start.5
  213.9 2.0 collective-permute-done.5
  215.9 3.5 collective-permute-done.4
  248.4 1.5 copy.118
  260.5 1.5 copy.122
  305.8 1.6 constant_dynamic-update-slice_fusion.25
  334.1 2.8 fusion.5
  338.6 8.2 %fusion.28 = f32[2,8,32,2048]{3,2,1,0:T(8,128)} fusion(bf16[64,2,8,32]{0,3,2,1:T(8,128)(2,1)S(1)} %copy.137, f32[2,8,64,2048]{3,2,1,0:T(8,128)} %copy-done.2, f32[2,8,64]{2,1,0:T(8,128)S(1)} %log_add_fusion, pred[64,2048]{1,0:T(8,128)(4,1)S(1)} %copy-done.12), kind=kOutput, calls=%fused_computation.156 | convolution fusion | flops 144703488 | bytes 12783616 | tf_op jit(solution)/shard_map/sbhak,asbhe->ksbhe/dot_general | solution.py:79
  346.8 7.2 multiply_convert_fusion
  354.0 5.4 copy.142
  359.4 5.0 convolution_multiply_fusion
  364.4 5.4 copy.141
  369.8 7.9 %pad_maximum_fusion = f32[2048,1,2,512]{3,0,2,1:T(8,128)} fusion(f32[2048,1,2,256]{3,0,2,1:T(8,128)} %copy.142, f32[2048,1,2,256]{3,0,2,1:T(8,128)} %copy.141), kind=kLoop, calls=%fused_computation | loop fusion | flops 2097152 | bytes 16777216 | tf_op jit(solution)/shard_map/concatenate | solution.py:199
  379.3 3.4 fusion.3
  385.0 145.6 %reduce-scatter.6.cloned.1.call-done = f32[64,1,2,512]{3,0,2,1:T(8,128)} async-done(((f32[2048,1,2,512]{3,0,2,1:T(8,128)}), f32[64,1,2,512]{3,0,2,1:T(8,128)}) %reduce-scatter.6.cloned.1.call-update) | async-done | bytes 262160 | tf_op jit(solution)/shard_map/reduce_scatter | solution.py:198
  535.8 3.9 bitcast_dynamic-update-slice_fusion
  541.6 150.0 %reduce-scatter.8.cloned.1.call-done = f32[8,31,256]{2,0,1:T(8,128)} async-done(((f32[256,31,256]{2,0,1:T(8,128)}), f32[8,31,256]{2,0,1:T(8,128)}) %reduce-scatter.8.cloned.1.call-update) | async-done | bytes 253968 | tf_op jit(solution)/shard_map/reduce_scatter | solution.py:225
  691.6 5.2 copy.159
  696.8 4.6 reshape.318
  701.4 1.8 fusion.33
  704.0 1.6 reshape.301
  705.6 1.7 copy.144
  707.3 1.6 reshape.302
  710.3 1.9 fusion.6
  713.7 27.2 %reduce-scatter.10.cloned.1.call-done = f32[32,248]{1,0:T(8,128)} async-done(((f32[256,248]{1,0:T(8,128)}), f32[32,248]{1,0:T(8,128)}) %reduce-scatter.10.cloned.1.call-update) | async-done | bytes 31760
  740.9 1.9 reshape.319
  742.8 2.0 copy.160
  (231 shorter events, 144.1 us)
Async XLA Ops:
  7.2 327.0 %copy-start = (bf16[256,27,256]{2,0,1:T(8,128)(2,1)S(1)}, bf16[256,27,256]{2,0,1:T(8,128)(2,1)}, u32[]{:S(2)}) copy-start(bf16[256,27,256]{2,0,1:T(8,128)(2,1)} %param.14) | copy-start | bytes 10616836
  7.2 86.8 %all-gather.5.cloned.1.call-start = ((), (), s32[]{:S(2)}) async-start(), calls=%async_computation.4 | async-start | bytes 2162688 | tf_op jit(solution)/shard_map/all_gather | solution.py:126
  12.1 161.6 %all-gather.3.cloned.1.call-start = ((), (), s32[]{:S(2)}) async-start(), calls=%async_computation.3 | async-start | bytes 2162688 | tf_op jit(solution)/shard_map/all_gather | solution.py:127
  15.4 515.2 %reduce-scatter.6.cloned.1.call-start = ((), (), s32[]{:S(2)}) async-start(), calls=%async_computation.5 | async-start | bytes 8650752 | tf_op jit(solution)/shard_map/reduce_scatter | solution.py:198
  100.2 3.5 copy-start.11
  103.6 3.3 copy-start.2
  194.4 0.6 copy-start.9
  196.3 2.6 collective-permute-start.1
  197.3 3.2 collective-permute-start
  201.5 4.4 collective-permute-start.3
  202.2 4.6 collective-permute-start.2
  206.0 0.8 copy-start.20
  206.8 1.7 copy-start.21
  208.4 7.5 collective-permute-start.5
  211.1 8.2 %collective-permute-start.4 = (bf16[2,66,1,4,256]{4,1,3,2,0:T(8,128)(2,1)}, bf16[2,66,1,4,256]{4,1,3,2,0:T(8,128)(2,1)}, u32[]{:S(2)}, u32[]{:S(2)}) collective-permute-start(bf16[2,66,1,4,256]{4,1,3,2,0:T(8,128)(2,1)} %pad_maximum_fusion.1), channel_id=1, source_target_pairs={{0,1},{1,2},{2,3},{3,0},{4,5},{5,6},{6,7},{7,4},{8,9},{9,10},{10,1... | collective-permute-start | bytes 811016 | tf_op jit(solution)/shard_map/ppermute | solution.py:19
  305.7 20.8 %copy-start.22 = (bf16[128,1,256]{2,0,1:T(8,128)(2,1)S(1)}, bf16[128,1,256]{2,0,1:T(8,128)(2,1)}, u32[]{:S(2)}) copy-start(bf16[128,1,256]{2,0,1:T(8,128)(2,1)} %stack.204) | copy-start | bytes 196612
  305.7 21.5 %copy-start.23 = (bf16[128,1,256]{2,0,1:T(8,128)(2,1)S(1)}, bf16[128,1,256]{2,0,1:T(8,128)(2,1)}, u32[]{:S(2)}) copy-start(bf16[128,1,256]{2,0,1:T(8,128)(2,1)} %stack.205) | copy-start | bytes 196612
  305.7 22.1 %copy-start.24 = (bf16[128,1,256]{2,0,1:T(8,128)(2,1)S(1)}, bf16[128,1,256]{2,0,1:T(8,128)(2,1)}, u32[]{:S(2)}) copy-start(bf16[128,1,256]{2,0,1:T(8,128)(2,1)} %stack.206) | copy-start | bytes 196612
  305.7 22.7 %copy-start.25 = (bf16[128,1,256]{2,0,1:T(8,128)(2,1)S(1)}, bf16[128,1,256]{2,0,1:T(8,128)(2,1)}, u32[]{:S(2)}) copy-start(bf16[128,1,256]{2,0,1:T(8,128)(2,1)} %stack.207) | copy-start | bytes 196612
  305.7 23.3 %copy-start.26 = (bf16[128,1,256]{2,0,1:T(8,128)(2,1)S(1)}, bf16[128,1,256]{2,0,1:T(8,128)(2,1)}, u32[]{:S(2)}) copy-start(bf16[128,1,256]{2,0,1:T(8,128)(2,1)} %stack.208) | copy-start | bytes 196612
  305.7 24.0 %copy-start.27 = (bf16[128,1,256]{2,0,1:T(8,128)(2,1)S(1)}, bf16[128,1,256]{2,0,1:T(8,128)(2,1)}, u32[]{:S(2)}) copy-start(bf16[128,1,256]{2,0,1:T(8,128)(2,1)} %stack.209) | copy-start | bytes 196612
  305.7 24.6 %copy-start.28 = (bf16[128,1,256]{2,0,1:T(8,128)(2,1)S(1)}, bf16[128,1,256]{2,0,1:T(8,128)(2,1)}, u32[]{:S(2)}) copy-start(bf16[128,1,256]{2,0,1:T(8,128)(2,1)} %stack.210) | copy-start | bytes 196612
  305.7 25.2 %copy-start.29 = (bf16[128,1,256]{2,0,1:T(8,128)(2,1)S(1)}, bf16[128,1,256]{2,0,1:T(8,128)(2,1)}, u32[]{:S(2)}) copy-start(bf16[128,1,256]{2,0,1:T(8,128)(2,1)} %stack.211) | copy-start | bytes 196612
  305.7 25.9 %copy-start.30 = (bf16[128,1,256]{2,0,1:T(8,128)(2,1)S(1)}, bf16[128,1,256]{2,0,1:T(8,128)(2,1)}, u32[]{:S(2)}) copy-start(bf16[128,1,256]{2,0,1:T(8,128)(2,1)} %stack.212) | copy-start | bytes 196612
  305.7 26.5 %copy-start.31 = (bf16[128,1,256]{2,0,1:T(8,128)(2,1)S(1)}, bf16[128,1,256]{2,0,1:T(8,128)(2,1)}, u32[]{:S(2)}) copy-start(bf16[128,1,256]{2,0,1:T(8,128)(2,1)} %stack.213) | copy-start | bytes 196612
  305.8 27.1 %copy-start.32 = (bf16[128,1,256]{2,0,1:T(8,128)(2,1)S(1)}, bf16[128,1,256]{2,0,1:T(8,128)(2,1)}, u32[]{:S(2)}) copy-start(bf16[128,1,256]{2,0,1:T(8,128)(2,1)} %stack.214) | copy-start | bytes 196612
  305.8 27.7 %copy-start.33 = (bf16[128,1,256]{2,0,1:T(8,128)(2,1)S(1)}, bf16[128,1,256]{2,0,1:T(8,128)(2,1)}, u32[]{:S(2)}) copy-start(bf16[128,1,256]{2,0,1:T(8,128)(2,1)} %stack.215) | copy-start | bytes 196612
  305.8 28.4 %copy-start.17 = (f32[128,256]{1,0:T(8,128)S(1)}, f32[128,256]{1,0:T(8,128)}, u32[]{:S(2)}) copy-start(f32[128,256]{1,0:T(8,128)} %reshape.309) | copy-start | bytes 393220
  334.1 3.4 copy-start.18
  336.9 0.7 copy-start.6
  337.6 0.9 copy-start.16
  337.6 1.0 copy-start.12
  338.6 8.2 %copy-start.8 = (bf16[2048,1,2,256]{0,3,2,1:T(8,128)(2,1)S(1)}, bf16[2048,1,2,256]{0,3,2,1:T(8,128)(2,1)}, u32[]{:S(2)}) copy-start(bf16[2048,1,2,256]{0,3,2,1:T(8,128)(2,1)} %copy.103) | copy-start | bytes 6291460
  354.0 5.4 copy-start.10
  377.7 1.6 copy-start.3
  377.7 5.5 copy-start.5
  377.7 313.9 %reduce-scatter.8.cloned.1.call-start = ((), (), s32[]{:S(2)}) async-start(), calls=%async_computation.6 | async-start | bytes 8380416 | tf_op jit(solution)/shard_map/reduce_scatter | solution.py:225
  382.7 1.7 copy-start.4
  384.3 146.3 %copy-start.15 = (bf16[64,1,2,256]{3,2,1,0:T(2,128)(2,1)S(1)}, bf16[64,1,2,256]{3,2,1,0:T(2,128)(2,1)}, u32[]{:S(2)}) copy-start(bf16[64,1,2,256]{3,2,1,0:T(2,128)(2,1)} %param.8) | copy-start | bytes 196612
  384.9 150.0 %copy-start.7 = (f32[128,256]{1,0:T(8,128)S(1)}, f32[128,256]{1,0:T(8,128)}, u32[]{:S(2)}) copy-start(f32[128,256]{1,0:T(8,128)} %copy-done.6) | copy-start | bytes 393220
  384.9 149.9 %copy-start.14 = (bf16[128,256]{1,0:T(8,128)(2,1)S(1)}, bf16[128,256]{1,0:T(8,128)(2,1)}, u32[]{:S(2)}) copy-start(bf16[128,256]{1,0:T(8,128)(2,1)} %convert_element_type.105) | copy-start | bytes 196612
  385.0 150.8 %copy-start.13 = (bf16[64,1,2,256]{3,2,1,0:T(2,128)(2,1)S(1)}, bf16[64,1,2,256]{3,2,1,0:T(2,128)(2,1)}, u32[]{:S(2)}) copy-start(bf16[64,1,2,256]{3,2,1,0:T(2,128)(2,1)} %param.9) | copy-start | bytes 196612
  539.7 0.9 copy-start.19
  539.7 201.2 %reduce-scatter.10.cloned.1.call-start = ((), (), s32[]{:S(2)}) async-start(), calls=%async_computation.7 | async-start | bytes 294912
  701.4 43.3 %copy-start.1 = (bf16[256,27,256]{2,0,1:T(8,128)(2,1)S(1)}, bf16[256,27,256]{2,0,1:T(8,128)(2,1)}, u32[]{:S(2)}) copy-start(bf16[256,27,256]{2,0,1:T(8,128)(2,1)} %param.14) | copy-start | bytes 10616836
Sparse Core Ops, SparseCore 0:
  12.2 81.6 all-gather.4
  97.3 76.3 all-gather.2
  377.8 152.7 reduce-scatter.5
  539.8 151.7 reduce-scatter.7
  701.6 39.3 reduce-scatter.9
where the time goes:
time: 756 us; the launch traced here: 751 us
  waiting for transfers between devices  471 us (62%)
  local copies, waits for them, and re-layouts  185 us (24%)
  matrix products  57.8 us (8%)
  other arithmetic  17.5 us (2%)
  between operations  14.4 us (2%)
    reduce_scatter x1, waiting for transfers between devices, per_device(): lax.psum_scatter(jnp.concatenate([projection_terms, conv_terms], axis=1),...  150 us
    reduce_scatter x1, waiting for transfers between devices, per_device(): lax.psum_scatter(jnp.concatenate([grad_key_part, grad_value_part], axis=3...  146 us
    all_gather x1, waiting for transfers between devices, per_device(): lax.all_gather(key_proj, 'azim', axis=0, tiled=True)  69.6 us
    all_gather x1, waiting for transfers between devices, per_device(): lax.all_gather(values, 'azim', axis=0, tiled=True)  66.8 us
    unnamed x129, local copies, waits for them, and re-layouts  51.9 us
    slice x29, local copies, waits for them, and re-layouts, gather_taps(): padded[first_at:first_at + col_count, second_at:second_at + sweeps, third...  42.1 us
    another operation x29, local copies, waits for them, and re-layouts, gather_taps(): return jnp.stack(pieces, axis=3)  41 us
    unnamed x6, waiting for transfers between devices  27.3 us
  transfers between devices with their start and end apart: 11, of which 11 were waited for; matrix products, arithmetic and copies ran while one was open for 6% of the time, Pallas kernels for 0%

commit v1 on v0

--- a/solution.py
+++ b/solution.py
@@ -123,7 +123,9 @@
     values = project(flat_in, w_value).reshape(features.shape)
     col_first = lax.axis_index("azim") * col_count
     key_all, value_all = (
-        lax.all_gather(key_proj, "azim", axis=0, tiled=True),
+        jnp.concatenate(
+            lax.all_to_all(jnp.stack([key_proj] * lax.axis_size("azim")), "azim", 0, 0), axis=0
+        ),
         lax.all_gather(values, "azim", axis=0, tiled=True),
     )
     allowed_all = allowed_table(sector_mask, col_first, col_count, 0, key_all.shape[0])

time: 756 us -> 698 us (0.923)
  waiting for transfers between devices: 471 us -> 390 us
  starting transfers between devices: 6.08 us -> 17.6 us
  local copies, waits for them, and re-layouts: 185 us -> 195 us
    all_gather x1 -> x0, waiting for transfers between devices: 69.6 us -> none  [per_device(): lax.all_gather(key_proj, 'azim', axis=0, tiled=True)]
    all_gather x1, waiting for transfers between devices: 66.8 us -> 13.1 us  [per_device(): lax.all_gather(values, 'azim', axis=0, tiled=True)]
    all_to_all x0 -> x1, waiting for transfers between devices: none -> 43.2 us  [per_device(): lax.all_to_all(jnp.stack([key_proj] * lax.axis_size('azim')), 'azim', 0, 0)]
    another operation x3 -> x9, local copies, waits for them, and re-layouts: 0.45 us -> 14.7 us
    all_to_all x0 -> x1, starting transfers between devices: none -> 11.4 us  [per_device(): lax.all_to_all(jnp.stack([key_proj] * lax.axis_size('azim')), 'azim', 0, 0)]
    unnamed x6 -> x5, waiting for transfers between devices: 27.3 us -> 27.3 us
  transfers between devices with their start and end apart: 11 -> 11, of which waited for: 11 -> 11; matrix products, arithmetic and copies ran while one was open for 6% -> 8% of each run, Pallas kernels for 0% -> 0%
where the time goes in v1:
time: 698 us; the launch traced here: 693 us
  waiting for transfers between devices  390 us (56%)
  local copies, waits for them, and re-layouts  195 us (28%)
  matrix products  57.8 us (8%)
  other arithmetic  17.7 us (3%)
  starting transfers between devices  17.6 us (3%)
  between operations  14.4 us (2%)
    reduce_scatter x1, waiting for transfers between devices, per_device(): lax.psum_scatter(jnp.concatenate([projection_terms, conv_terms], axis=1),...  150 us
    reduce_scatter x1, waiting for transfers between devices, per_device(): lax.psum_scatter(jnp.concatenate([grad_key_part, grad_value_part], axis=3...  145 us
    unnamed x129, local copies, waits for them, and re-layouts  51.6 us
    all_to_all x1, waiting for transfers between devices, per_device(): lax.all_to_all(jnp.stack([key_proj] * lax.axis_size('azim')), 'azim', 0, 0)  43.2 us
    slice x29, local copies, waits for them, and re-layouts, gather_taps(): padded[first_at:first_at + col_count, second_at:second_at + sweeps, third...  42.5 us
    another operation x29, local copies, waits for them, and re-layouts, gather_taps(): return jnp.stack(pieces, axis=3)  40.9 us
    unnamed x5, waiting for transfers between devices  27.3 us
  transfers between devices with their start and end apart: 11, of which 11 were waited for; matrix products, arithmetic and copies ran while one was open for 8% of the time, Pallas kernels for 0%

profile of v1, /device:TPU:32, one launch (start us, length us, event | category | flops | bytes accessed | tf_op | source)
XLA Modules:
  0.0 693.2 jit_solution(17774769650930524653)
XLA Ops:
  7.2 1.6 reshape.288
  8.8 1.7 convolution_convert_fusion.2
  12.9 1.6 stack.190
  14.5 11.4 %all-to-all-start = ((bf16[32,64,1,2,256]{4,1,3,2,0:T(8,128)(2,1)}), bf16[32,64,1,2,256]{4,1,3,2,0:T(8,128)(2,1)}, u32[]{:S(2)}, u32[]{:S(2)}) async-start(bf16[32,64,1,2,256]{4,1,3,2,0:T(8,128)(2,1)} %stack.190), calls=%async_computation | async-start | bytes 4194304 | tf_op jit(solution)/shard_map/all_to_all | solution.py:127
  26.0 1.7 convolution_convert_fusion.4
  30.8 1.7 convolution_convert_fusion.3
  32.5 1.8 reshape.291
  34.3 1.8 copy.106
  36.1 2.0 convolution_compare_fusion
  38.2 43.2 %all-to-all-done = bf16[32,64,1,2,256]{4,1,3,2,0:T(8,128)(2,1)} async-done(((bf16[32,64,1,2,256]{4,1,3,2,0:T(8,128)(2,1)}), bf16[32,64,1,2,256]{4,1,3,2,0:T(8,128)(2,1)}, u32[]{:S(2)}, u32[]{:S(2)}) %all-to-all-start) | async-done | bytes 2097184 | tf_op jit(solution)/shard_map/all_to_all | solution.py:127
  81.4 7.4 %copy.105 = bf16[32,64,1,2,256]{1,0,4,3,2:T(8,128)(2,1)} copy(bf16[32,64,1,2,256]{4,1,3,2,0:T(8,128)(2,1)} %all-to-all-done) | data formatting | bytes 4194304 | tf_op jit(solution)/shard_map/all_to_all | solution.py:127
  88.8 6.7 reshape.292
  95.6 3.5 fusion.1
  99.1 2.2 exponential_reduce_fusion
  102.4 13.1 %all-gather.2.cloned.1.call-done = bf16[2048,1,2,256]{3,2,1,0:T(2,128)(2,1)} async-done(((bf16[64,1,2,256]{3,2,1,0:T(2,128)(2,1)}), bf16[2048,1,2,256]{3,2,1,0:T(2,128)(2,1)}) %all-gather.2.cloned.1.call-update) | async-done | bytes 2097168 | tf_op jit(solution)/shard_map/all_gather | solution.py:129
  115.5 6.2 copy.103
  121.7 6.8 convolution_convert_fusion
  128.5 1.8 copy.107
  130.3 1.8 convert_element_type.105
  132.1 1.7 fusion.7
  140.7 1.7 collective-permute-done
  146.3 1.7 collective-permute-done.3
  148.8 1.7 pad_maximum_fusion.1
  150.4 2.7 collective-permute-start.5
  156.0 1.9 collective-permute-done.5
  157.9 3.5 collective-permute-done.4
  248.0 1.6 constant_dynamic-update-slice_fusion.25
  276.1 2.8 fusion.5
  280.6 8.2 %fusion.28 = f32[2,8,32,2048]{3,2,1,0:T(8,128)} fusion(bf16[64,2,8,32]{0,3,2,1:T(8,128)(2,1)S(1)} %copy.137, f32[2,8,64,2048]{3,2,1,0:T(8,128)} %copy-done.2, f32[2,8,64]{2,1,0:T(8,128)S(1)} %log_add_fusion, pred[64,2048]{1,0:T(8,128)(4,1)S(1)} %copy-done.12), kind=kOutput, calls=%fused_computation.156 | convolution fusion | flops 144703488 | bytes 12783616 | tf_op jit(solution)/shard_map/sbhak,asbhe->ksbhe/dot_general | solution.py:79
  288.8 7.2 %multiply_convert_fusion = bf16[2,8,64,2048]{3,2,1,0:T(8,128)(2,1)} fusion(f32[2,8,64,2048]{3,2,1,0:T(8,128)} %copy-done.2, bf16[64,2,8,32]{0,3,2,1:T(8,128)(2,1)S(1)} %copy.137, bf16[2048,2,8,32]{0,3,2,1:T(8,128)(2,1)S(1)} %bitcast.297, f32[2,8,64]{2,1,0:T(8,128)S(1)} %multiply_reduce_fusion, f32[2,8,64]{2,1,0:T(8,128)S(1)} %log_add_fusion, ...), kind=kOutput, calls=%fused_computation.1 | convolution fusion | flops 148897792 | bytes 14884864 | tf_op jit(solution)/shard_map/asbhe,ksbhe->sbhak/dot_general | solution.py:176
  296.0 5.4 copy.142
  301.4 5.0 convolution_multiply_fusion
  306.4 5.4 copy.141
  311.8 7.9 %pad_maximum_fusion = f32[2048,1,2,512]{3,0,2,1:T(8,128)} fusion(f32[2048,1,2,256]{3,0,2,1:T(8,128)} %copy.142, f32[2048,1,2,256]{3,0,2,1:T(8,128)} %copy.141), kind=kLoop, calls=%fused_computation | loop fusion | flops 2097152 | bytes 16777216 | tf_op jit(solution)/shard_map/concatenate | solution.py:201
  321.3 3.4 fusion.3
  327.1 145.4 %reduce-scatter.6.cloned.1.call-done = f32[64,1,2,512]{3,0,2,1:T(8,128)} async-done(((f32[2048,1,2,512]{3,0,2,1:T(8,128)}), f32[64,1,2,512]{3,0,2,1:T(8,128)}) %reduce-scatter.6.cloned.1.call-update) | async-done | bytes 262160 | tf_op jit(solution)/shard_map/reduce_scatter | solution.py:200
  477.6 3.9 bitcast_dynamic-update-slice_fusion
  483.4 150.1 %reduce-scatter.8.cloned.1.call-done = f32[8,31,256]{2,0,1:T(8,128)} async-done(((f32[256,31,256]{2,0,1:T(8,128)}), f32[8,31,256]{2,0,1:T(8,128)}) %reduce-scatter.8.cloned.1.call-update) | async-done | bytes 253968 | tf_op jit(solution)/shard_map/reduce_scatter | solution.py:227
  633.5 5.2 copy.159
  638.7 4.6 reshape.315
  643.4 1.8 fusion.33
  645.9 1.6 reshape.298
  647.6 1.7 copy.144
  649.2 1.6 reshape.299
  652.2 1.9 fusion.6
  655.6 27.3 %reduce-scatter.10.cloned.1.call-done = f32[32,248]{1,0:T(8,128)} async-done(((f32[256,248]{1,0:T(8,128)}), f32[32,248]{1,0:T(8,128)}) %reduce-scatter.10.cloned.1.call-update) | async-done | bytes 31760
  682.8 1.9 reshape.316
  684.7 2.0 copy.160
  (233 shorter events, 149.8 us)
Async XLA Ops:
  7.2 269.0 %copy-start = (bf16[256,27,256]{2,0,1:T(8,128)(2,1)S(1)}, bf16[256,27,256]{2,0,1:T(8,128)(2,1)}, u32[]{:S(2)}) copy-start(bf16[256,27,256]{2,0,1:T(8,128)(2,1)} %param.14) | copy-start | bytes 10616836
  14.5 66.9 %all-to-all-start = ((bf16[32,64,1,2,256]{4,1,3,2,0:T(8,128)(2,1)}), bf16[32,64,1,2,256]{4,1,3,2,0:T(8,128)(2,1)}, u32[]{:S(2)}, u32[]{:S(2)}) async-start(bf16[32,64,1,2,256]{4,1,3,2,0:T(8,128)(2,1)} %stack.190), calls=%async_computation | async-start | bytes 4194304 | tf_op jit(solution)/shard_map/all_to_all | solution.py:127
  25.9 89.5 %all-gather.2.cloned.1.call-start = ((), (), s32[]{:S(2)}) async-start(), calls=%async_computation.4 | async-start | bytes 2162688 | tf_op jit(solution)/shard_map/all_gather | solution.py:129
  29.3 443.2 %reduce-scatter.6.cloned.1.call-start = ((), (), s32[]{:S(2)}) async-start(), calls=%async_computation.5 | async-start | bytes 8650752 | tf_op jit(solution)/shard_map/reduce_scatter | solution.py:200
  95.6 3.5 copy-start.11
  99.1 3.3 copy-start.2
  136.2 0.6 copy-start.9
  138.1 2.6 collective-permute-start.1
  139.2 3.2 collective-permute-start
  143.4 4.6 collective-permute-start.3
  144.2 4.6 collective-permute-start.2
  148.0 0.8 copy-start.20
  148.8 1.7 copy-start.21
  150.4 7.5 %collective-permute-start.5 = (bf16[2,66,1,4,256]{4,1,3,2,0:T(8,128)(2,1)}, bf16[2,66,1,4,256]{4,1,3,2,0:T(8,128)(2,1)}, u32[]{:S(2)}, u32[]{:S(2)}) collective-permute-start(bf16[2,66,1,4,256]{4,1,3,2,0:T(8,128)(2,1)} %pad_maximum_fusion.1), channel_id=1, source_target_pairs={{1,0},{2,1},{3,2},{0,3},{5,4},{6,5},{7,6},{4,7},{9,8},{10,9},{11,1... | collective-permute-start | bytes 811016 | tf_op jit(solution)/shard_map/ppermute | solution.py:22
  153.1 8.2 %collective-permute-start.4 = (bf16[2,66,1,4,256]{4,1,3,2,0:T(8,128)(2,1)}, bf16[2,66,1,4,256]{4,1,3,2,0:T(8,128)(2,1)}, u32[]{:S(2)}, u32[]{:S(2)}) collective-permute-start(bf16[2,66,1,4,256]{4,1,3,2,0:T(8,128)(2,1)} %pad_maximum_fusion.1), channel_id=1, source_target_pairs={{0,1},{1,2},{2,3},{3,0},{4,5},{5,6},{6,7},{7,4},{8,9},{9,10},{10,1... | collective-permute-start | bytes 811016 | tf_op jit(solution)/shard_map/ppermute | solution.py:19
  247.9 20.7 %copy-start.22 = (bf16[128,1,256]{2,0,1:T(8,128)(2,1)S(1)}, bf16[128,1,256]{2,0,1:T(8,128)(2,1)}, u32[]{:S(2)}) copy-start(bf16[128,1,256]{2,0,1:T(8,128)(2,1)} %stack.208) | copy-start | bytes 196612
  247.9 21.3 %copy-start.23 = (bf16[128,1,256]{2,0,1:T(8,128)(2,1)S(1)}, bf16[128,1,256]{2,0,1:T(8,128)(2,1)}, u32[]{:S(2)}) copy-start(bf16[128,1,256]{2,0,1:T(8,128)(2,1)} %stack.209) | copy-start | bytes 196612
  247.9 21.9 %copy-start.24 = (bf16[128,1,256]{2,0,1:T(8,128)(2,1)S(1)}, bf16[128,1,256]{2,0,1:T(8,128)(2,1)}, u32[]{:S(2)}) copy-start(bf16[128,1,256]{2,0,1:T(8,128)(2,1)} %stack.210) | copy-start | bytes 196612
  247.9 22.5 %copy-start.25 = (bf16[128,1,256]{2,0,1:T(8,128)(2,1)S(1)}, bf16[128,1,256]{2,0,1:T(8,128)(2,1)}, u32[]{:S(2)}) copy-start(bf16[128,1,256]{2,0,1:T(8,128)(2,1)} %stack.211) | copy-start | bytes 196612
  247.9 23.2 %copy-start.26 = (bf16[128,1,256]{2,0,1:T(8,128)(2,1)S(1)}, bf16[128,1,256]{2,0,1:T(8,128)(2,1)}, u32[]{:S(2)}) copy-start(bf16[128,1,256]{2,0,1:T(8,128)(2,1)} %stack.212) | copy-start | bytes 196612
  248.0 23.8 %copy-start.27 = (bf16[128,1,256]{2,0,1:T(8,128)(2,1)S(1)}, bf16[128,1,256]{2,0,1:T(8,128)(2,1)}, u32[]{:S(2)}) copy-start(bf16[128,1,256]{2,0,1:T(8,128)(2,1)} %stack.213) | copy-start | bytes 196612
  248.0 24.4 %copy-start.28 = (bf16[128,1,256]{2,0,1:T(8,128)(2,1)S(1)}, bf16[128,1,256]{2,0,1:T(8,128)(2,1)}, u32[]{:S(2)}) copy-start(bf16[128,1,256]{2,0,1:T(8,128)(2,1)} %stack.214) | copy-start | bytes 196612
  248.0 25.0 %copy-start.29 = (bf16[128,1,256]{2,0,1:T(8,128)(2,1)S(1)}, bf16[128,1,256]{2,0,1:T(8,128)(2,1)}, u32[]{:S(2)}) copy-start(bf16[128,1,256]{2,0,1:T(8,128)(2,1)} %stack.215) | copy-start | bytes 196612
  248.0 25.6 %copy-start.30 = (bf16[128,1,256]{2,0,1:T(8,128)(2,1)S(1)}, bf16[128,1,256]{2,0,1:T(8,128)(2,1)}, u32[]{:S(2)}) copy-start(bf16[128,1,256]{2,0,1:T(8,128)(2,1)} %stack.216) | copy-start | bytes 196612
  248.0 26.3 %copy-start.31 = (bf16[128,1,256]{2,0,1:T(8,128)(2,1)S(1)}, bf16[128,1,256]{2,0,1:T(8,128)(2,1)}, u32[]{:S(2)}) copy-start(bf16[128,1,256]{2,0,1:T(8,128)(2,1)} %stack.217) | copy-start | bytes 196612
  248.0 26.9 %copy-start.32 = (bf16[128,1,256]{2,0,1:T(8,128)(2,1)S(1)}, bf16[128,1,256]{2,0,1:T(8,128)(2,1)}, u32[]{:S(2)}) copy-start(bf16[128,1,256]{2,0,1:T(8,128)(2,1)} %stack.218) | copy-start | bytes 196612
  248.0 27.5 %copy-start.33 = (bf16[128,1,256]{2,0,1:T(8,128)(2,1)S(1)}, bf16[128,1,256]{2,0,1:T(8,128)(2,1)}, u32[]{:S(2)}) copy-start(bf16[128,1,256]{2,0,1:T(8,128)(2,1)} %stack.219) | copy-start | bytes 196612
  248.0 28.1 %copy-start.17 = (f32[128,256]{1,0:T(8,128)S(1)}, f32[128,256]{1,0:T(8,128)}, u32[]{:S(2)}) copy-start(f32[128,256]{1,0:T(8,128)} %reshape.306) | copy-start | bytes 393220
  276.1 3.5 copy-start.18
  278.9 0.7 copy-start.6
  279.6 0.9 copy-start.16
  279.6 1.0 copy-start.12
  280.6 8.2 %copy-start.8 = (bf16[2048,1,2,256]{0,3,2,1:T(8,128)(2,1)S(1)}, bf16[2048,1,2,256]{0,3,2,1:T(8,128)(2,1)}, u32[]{:S(2)}) copy-start(bf16[2048,1,2,256]{0,3,2,1:T(8,128)(2,1)} %copy.103) | copy-start | bytes 6291460
  296.0 5.4 copy-start.10
  319.7 1.6 copy-start.3
  319.7 5.5 copy-start.5
  319.7 313.8 %reduce-scatter.8.cloned.1.call-start = ((), (), s32[]{:S(2)}) async-start(), calls=%async_computation.6 | async-start | bytes 8380416 | tf_op jit(solution)/shard_map/reduce_scatter | solution.py:227
  324.7 1.7 copy-start.4
  326.4 146.1 %copy-start.15 = (bf16[64,1,2,256]{3,2,1,0:T(2,128)(2,1)S(1)}, bf16[64,1,2,256]{3,2,1,0:T(2,128)(2,1)}, u32[]{:S(2)}) copy-start(bf16[64,1,2,256]{3,2,1,0:T(2,128)(2,1)} %param.8) | copy-start | bytes 196612
  326.9 149.7 %copy-start.7 = (f32[128,256]{1,0:T(8,128)S(1)}, f32[128,256]{1,0:T(8,128)}, u32[]{:S(2)}) copy-start(f32[128,256]{1,0:T(8,128)} %copy-done.6) | copy-start | bytes 393220
  326.9 149.7 %copy-start.14 = (bf16[128,256]{1,0:T(8,128)(2,1)S(1)}, bf16[128,256]{1,0:T(8,128)(2,1)}, u32[]{:S(2)}) copy-start(bf16[128,256]{1,0:T(8,128)(2,1)} %convert_element_type.105) | copy-start | bytes 196612
  327.1 150.5 %copy-start.13 = (bf16[64,1,2,256]{3,2,1,0:T(2,128)(2,1)S(1)}, bf16[64,1,2,256]{3,2,1,0:T(2,128)(2,1)}, u32[]{:S(2)}) copy-start(bf16[64,1,2,256]{3,2,1,0:T(2,128)(2,1)} %param.9) | copy-start | bytes 196612
  481.5 0.9 copy-start.19
  481.5 201.3 %reduce-scatter.10.cloned.1.call-start = ((), (), s32[]{:S(2)}) async-start(), calls=%async_computation.7 | async-start | bytes 294912
  643.4 43.3 %copy-start.1 = (bf16[256,27,256]{2,0,1:T(8,128)(2,1)S(1)}, bf16[256,27,256]{2,0,1:T(8,128)(2,1)}, u32[]{:S(2)}) copy-start(bf16[256,27,256]{2,0,1:T(8,128)(2,1)} %param.14) | copy-start | bytes 10616836
Sparse Core Ops, SparseCore 0:
  30.1 85.3 all-gather.1
  319.9 152.6 reduce-scatter.5
  481.7 151.8 reduce-scatter.7
  643.5 39.3 reduce-scatter.9
